TPU v7x, 256 devices: a whole 4x4x8 slice. The times are simulated.
256 devices in a mesh: tile: 32 (over z_hi, y, core), lev: 8 (over x, z_lo).
Axes of the slice: x: 4, y: 4, z: 8 (z_hi: 4, z_lo: 2; z = z_hi * 2 + z_lo), core: 2. Of those that a mesh axis runs over, the one named last changes fastest.
Arguments:
- tracer_start: float32 [48, 2048, 720], P('lev', 'tile'), may hold values from -6 to 6
- wind_row: float32 [48, 2048, 720], P('lev', 'tile'), may hold values from -0.16 to 0.16
- wind_col: float32 [48, 2048, 720], P('lev', 'tile'), may hold values from -0.16 to 0.16
- diffusivity: float32 [48, 2048, 720], P('lev', 'tile'), may hold values from 0.01 to 0.16
- flux: float32 [11520, 128], P(('tile', 'lev')), may hold values from -6 to 6
- remap_weights: float32 [23040, 128, 128], P(('tile', 'lev')), may hold values from -0.5 to 0.5
- remap_tile: int32 [23040, 1], P(('tile', 'lev')), may hold values from 0 to 31; in each aligned block of 90 rows (0 to 89, 90 to 179, ...) at most 8 rows name the same one
- remap_block: int32 [23040], P(('tile', 'lev')), may hold values from 0 to 359
- profiles: float32 [64, 48], P(None, 'lev'), may hold values from -0.875 to 0.875
- sound_count: int32 [32], P('tile'), may hold values from 1 to 2048, 32768 in all
- sound_col: int32 [65536], P('tile'), may hold values from 0 to 46079
- sound_prof: int32 [65536], P('tile'), may hold values from 0 to 63
- sound_obs: float32 [65536], P('tile'), may hold values from -8 to 8
- sound_sigma: float32 [65536], P('tile'), may hold values from 0.5 to 2
Outputs:
- modeled: float32 [65536], P('tile')
- misfit: float32 [65536], P('tile')
- state_gradient: float32 [48, 2048, 720], P('lev', 'tile')
- flux_gradient: float32 [11520, 128], P(('tile', 'lev'))
Inputs may be any that keep to these rules, and one draw needn't show every extreme that they name: `remap_tile`: within the (90) entries of one device no tile is named more than 8 times, a bound that some block reaches. `sound_count`: some tile has exactly 2048 live soundings.
All inputs are finite; a program needn't handle non-finite values. No bound on the sum of `sound_count` on one device may be relied on, other than what follows from the above.
Results may differ from a plain program's by a relative error of at most 0.0003.
Values sent between devices are 32-bit elements; how exact they have to be, the bound alone decides.
A program may use at most 128 MiB of HBM per device.

v0:
```python
import jax
import jax.numpy as jnp
from jax import lax
from jax.sharding import PartitionSpec as P

highest = lax.Precision.HIGHEST


def with_halo(cells, sides, width):
    for axis, dim in sides:
        count = lax.axis_size(axis)
        ends = count - 1
        head = lax.slice_in_dim(cells, 0, width, axis=dim)
        tail = lax.slice_in_dim(cells, cells.shape[dim] - width, cells.shape[dim], axis=dim)
        cells = jnp.concatenate(
            [
                lax.ppermute(tail, axis, [(i, (i + 1) % count) for i in range(ends)]),
                cells,
                lax.ppermute(head, axis, [((i + 1) % count, i) for i in range(ends)]),
            ],
            axis=dim,
        )
    return cells


def from_behind(value, axis, steps):
    count = lax.axis_size(axis)
    leading, last = (max(0, -steps), min(count, count - steps))
    return lax.ppermute(value, axis, [(source, source + steps) for source in range(leading, last)])


def spread(block, axis, holder):
    block = jnp.where(lax.axis_index(axis) == holder, block, jnp.zeros_like(block))
    return lax.psum(block, axis)


def apply_step(field, above, below, upper, lower, coeffs, adjoint):
    rise, rise_low, cross, cross_left, mixing, mixing_low = coeffs
    right = jnp.roll(field, -1, axis=2)
    left = jnp.roll(field, 1, axis=2)
    rise_pos = jnp.maximum(rise, 0.0)
    rise_neg = jnp.minimum(rise, 0.0)
    low_pos = jnp.maximum(rise_low, 0.0)
    low_neg = jnp.minimum(rise_low, 0.0)
    cross_pos = jnp.maximum(cross, 0.0)
    cross_neg = jnp.minimum(cross, 0.0)
    left_pos = jnp.maximum(cross_left, 0.0)
    left_neg = jnp.minimum(cross_left, 0.0)
    diffusion = mixing * (above - field) - mixing_low * (field - below)
    if adjoint:
        rows_term = rise_pos * (upper - field) - low_neg * (lower - field)
        cols_term = cross_pos * (right - field) - left_neg * (left - field)
    else:
        rows_term = low_pos * lower + low_neg * field - rise_pos * field - rise_neg * upper
        cols_term = left_pos * left + left_neg * field - cross_pos * field - cross_neg * right
    return field + rows_term + cols_term + diffusion


def transport(field, coeffs, adjoint):
    padded = with_halo(field, (("tile", 1), ("lev", 0)), 1)
    above = padded[2:, 1:-1, :]
    below = padded[:-2, 1:-1, :]
    upper = padded[1:-1, 2:, :]
    lower = padded[1:-1, :-2, :]
    return apply_step(field, above, below, upper, lower, coeffs, adjoint)


def on_device(
    tracer_start,
    wind_row,
    wind_col,
    diffusivity,
    flux,
    remap_weights,
    remap_tile,
    remap_block,
    profiles,
    sound_count,
    sound_col,
    sound_prof,
    sound_obs,
    sound_sigma,
):
    levels, rows, cols = tracer_start.shape
    entries, block_size, flux_cells = remap_weights.shape
    blocks = rows * cols // block_size
    tiles = lax.axis_size("tile")
    tile_index = lax.axis_index("tile")
    lev_index = lax.axis_index("lev")
    row_ids = lax.broadcasted_iota(jnp.int32, (1, rows, 1), 1)
    top_row = (row_ids == rows - 1) & (tile_index == tiles - 1)
    rise = jnp.where(top_row, 0.0, wind_row)
    rise_edge = from_behind(rise[:, rows - 1, :], "tile", 1)
    rise_low = jnp.concatenate([rise_edge[:, None, :], rise[:, : rows - 1, :]], axis=1)
    level_ids = lax.broadcasted_iota(jnp.int32, (levels, 1, 1), 0)
    top_level = (level_ids == levels - 1) & (lev_index == lax.axis_size("lev") - 1)
    mixing = jnp.where(top_level, 0.0, diffusivity)
    mixing_edge = from_behind(mixing[levels - 1], "lev", 1)
    mixing_low = jnp.concatenate([mixing_edge[None], mixing[: levels - 1]], axis=0)
    cross_left = jnp.roll(wind_col, 1, axis=2)
    coeffs = (rise, rise_low, wind_col, cross_left, mixing, mixing_low)
    flux_rep = jnp.repeat(flux, 2, axis=0)
    contrib = jnp.einsum(
        "ecf,ef->ec", remap_weights, flux_rep, precision=highest, preferred_element_type=jnp.float32
    )
    target = remap_tile[:, 0]
    global_rows = target * blocks + remap_block
    count = lax.axis_size("tile") * blocks
    local = global_rows
    inside = (local >= 0) & (local < count)
    summed = jax.ops.segment_sum(contrib, jnp.where(inside, local, count), num_segments=count + 1)
    partial_value = lax.psum_scatter(summed[:count], "tile", scatter_dimension=0, tiled=True)
    state = transport(tracer_start, coeffs, False)
    surface = lax.psum(partial_value, "lev").reshape(rows, cols)
    emission = jnp.where(lev_index == 0, surface, 0.0)
    state = state.at[0].add(emission)
    state = transport(state, coeffs, False)
    state = state.at[0].add(emission)
    slots = sound_col.shape[0]
    live = lax.iota(jnp.int32, slots) < sound_count[0]
    chooser = (sound_prof[:, None] == lax.iota(jnp.int32, profiles.shape[0])[None, :]).astype(
        jnp.float32
    )
    weights = jnp.dot(chooser, profiles, precision=highest, preferred_element_type=jnp.float32)
    flat = state.reshape(levels, rows * cols)
    values = jnp.take(flat, sound_col, axis=1)
    partial_column = jnp.sum(weights * values.T, axis=1)
    column = lax.psum(partial_column, "lev")
    modeled = jnp.where(live, column, 0.0)
    scaled = (column - sound_obs) / sound_sigma
    size_abs = jnp.abs(scaled)
    huber = jnp.where(size_abs <= 1.0, 0.5 * scaled * scaled, size_abs - 0.5)
    misfit = jnp.where(live, huber, 0.0)
    slope = jnp.where(live, jnp.clip(scaled, -1.0, 1.0) / sound_sigma, 0.0)
    adjoint_two = (
        jnp.zeros((levels, rows * cols), jnp.float32)
        .at[:, sound_col]
        .add((weights * slope[:, None]).T)
    )
    adjoint_two = adjoint_two.reshape(levels, rows, cols)
    adjoint_one = transport(adjoint_two, coeffs, True)
    surface_bar = (adjoint_two[0] + adjoint_one[0]).reshape(blocks, block_size)
    shared = spread(surface_bar, "lev", 0)
    piece = lax.all_gather(shared, "tile", axis=0, tiled=True)
    local = global_rows
    inside = (local >= 0) & (local < piece.shape[0])
    found = piece[jnp.clip(local, 0, piece.shape[0] - 1)]
    picked = jnp.where(inside[:, None], found, 0.0)
    state_gradient = transport(adjoint_one, coeffs, True)
    per_entry = jnp.einsum(
        "ecf,ec->ef", remap_weights, picked, precision=highest, preferred_element_type=jnp.float32
    )
    flux_gradient = per_entry.reshape(-1, 2, flux_cells).sum(axis=1)
    return (modeled, misfit, state_gradient, flux_gradient)


def solution(mesh):
    in_specs = (
        P("lev", "tile", None),
        P("lev", "tile", None),
        P("lev", "tile", None),
        P("lev", "tile", None),
        P(("tile", "lev"), None),
        P(("tile", "lev"), None, None),
        P(("tile", "lev"), None),
        P(("tile", "lev")),
        P(None, "lev"),
        P("tile"),
        P("tile"),
        P("tile"),
        P("tile"),
        P("tile"),
    )
    out_specs = (P("tile"), P("tile"), P("lev", "tile", None), P(("tile", "lev"), None))
    return jax.shard_map(
        on_device, mesh=mesh, in_specs=in_specs, out_specs=out_specs, check_vma=False
    )
```

profile of v0, /device:TPU:1, one launch (start us, length us, event | category | flops | bytes accessed | tf_op | source)
XLA Modules:
  0.0 527.5 jit_solution(2005856209609383764)
XLA Ops:
  8.4 11.2 %fusion.93 = f32[90,1,128]{2,1,0:T(1,128)S(1)} fusion(f32[90,128,128]{2,1,0:T(8,128)} %param.23, f32[90,128,1]{1,2,0:T(1,128)S(1)} %bitcast.55), kind=kOutput, calls=%fused_computation.180 | convolution fusion | flops 17694720 | bytes 5990400 | tf_op jit(solution)/shard_map/ecf,ef->ec/dot_general | solution.py:103
  19.6 3.8 scatter_custom_fusion
  23.3 4.5 slice.304
  27.9 1.7 fusion.92
  29.6 4.6 collective-permute-start.1
  34.2 2.4 collective-permute-start.2
  36.9 3.3 collective-permute-start
  41.1 3.5 collective-permute-start.4
  45.5 1.8 fusion.90
  48.7 1.4 collective-permute-start.3
  50.1 4.0 collective-permute-start.5
  57.8 76.1 %reduce-scatter.4.cloned.1.call-done = f32[360,128]{1,0:T(8,128)} async-done(((f32[11520,128]{1,0:T(8,128)}), f32[360,128]{1,0:T(8,128)}) %reduce-scatter.4.cloned.1.call-update) | async-done | bytes 184336
  134.9 6.5 %fusion.46 = f32[6,64,720]{2,1,0:T(8,128)S(1)} fusion(f32[6,64,720]{2,1,0:T(8,128)} %param.18, f32[1,66,720]{2,1,0:T(8,128)} %copy-done.30, f32[6,1,720]{2,1,0:T(1,128)} %collective-permute-done.2, f32[6,1,720]{2,1,0:T(1,128)} %collective-permute-done.1, f32[1,66,720]{2,1,0:T(8,128)} %copy-done.29, f32[6,64,719]{2,1,0:T(8,128)} %get-tuple-element.55, ...), kind=kLoop, calls=%fused_computation.76 | loop fusion | flops 12441600 | bytes 11473990 | tf_op jit(solution)/shard_map/add | solution.py:56
  141.4 67.9 %all-reduce.4.cloned.1.call-done = f32[360,128]{1,0:T(8,128)} async-done(((f32[360,128]{1,0:T(8,128)}), f32[360,128]{1,0:T(8,128)}) %all-reduce.4.cloned.1.call-update) | async-done | bytes 184336 | tf_op jit(solution)/shard_map/psum | solution.py:114
  209.3 1.6 broadcast_select_fusion.2
  210.9 1.8 select_n.77
  213.7 9.0 %collective-permute-start.6 = (f32[6,1,720]{2,1,0:T(1,128)S(1)}, f32[6,1,720]{2,1,0:T(1,128)S(1)}, u32[]{:S(2)}, u32[]{:S(2)}) collective-permute-start(f32[6,1,720]{2,1,0:T(1,128)S(1)} %get-tuple-element.52), channel_id=1, source_target_pairs={{0,8},{8,16},{16,24},{24,32},{32,40},{40,48},{48,56},{56,64},{64,7... | collective-permute-start | bytes 51848 | tf_op jit(solution)/shard_map/ppermute | solution.py:17
  222.7 1.9 collective-permute-start.7
  225.1 2.7 collective-permute-done.7
  227.8 1.3 collective-permute-start.8
  229.1 4.0 collective-permute-start.9
  233.2 3.6 collective-permute-done.8
  237.1 3.6 fusion.33
  240.7 1.6 fusion.70
  242.3 11.9 %copy.79 = f32[6,64,720]{0,2,1:T(8,128)} copy(f32[6,64,720]{2,1,0:T(8,128)} %fusion.70) | data formatting | bytes 2211840 | tf_op jit(solution)/shard_map/scatter-add | solution.py:118
  254.3 13.2 %gather_fusion = f32[2048,6]{1,0:T(8,128)S(1)} fusion(f32[6,46080]{0,1:T(8,128)} %bitcast.49, s32[2048]{0:T(1024)S(1)} %get-tuple-element.64), kind=kCustom, calls=%fused_computation | custom fusion | bytes 106496 | tf_op jit(solution)/shard_map/jit(_take)/gather | solution.py:126
  268.8 15.9 %psum.22 = f32[2048]{0:T(1024)S(1)} all-reduce(f32[2048]{0:T(1024)S(1)} %get-tuple-element.67), channel_id=1, replica_groups=mesh['tile'=32,'lev'=8] {'lev'}, use_global_device_ids=true, to_apply=%region_4.5 | all-reduce | flops 2048 | bytes 16384 | tf_op jit(solution)/shard_map/psum | solution.py:128
  285.8 20.8 %scatter_custom_fusion.1 = f32[6,46080]{0,1:T(8,128)} fusion(s32[2048]{0:T(1024)} %get-tuple-element.63, f32[2048,6]{1,0:T(8,128)S(1)} %copy.81, f32[]{:T(128)} %constant.93.clone.1), kind=kCustom, calls=%fused_computation.5 | custom fusion | flops 12288 | bytes 1106432 | tf_op jit(solution)/shard_map/scatter-add | solution.py:138
  306.6 11.9 %slice_reduce_fusion = f32[46080]{0:T(1024)} fusion(f32[6,46080]{0,1:T(8,128)} %scatter_custom_fusion.1), kind=kLoop, calls=%fused_computation.4 | loop fusion | bytes 368640 | tf_op jit(solution)/shard_map/slice | solution.py:142
  318.5 12.5 %copy.88 = f32[6,64,720]{2,1,0:T(8,128)S(1)} copy(f32[6,64,720]{0,2,1:T(8,128)} %bitcast.40) | data formatting | bytes 2211840 | tf_op jit(solution)/shard_map/reshape | solution.py:140
  331.1 7.2 %collective-permute-start.11 = (f32[6,1,720]{2,1,0:T(1,128)S(1)}, f32[6,1,720]{2,1,0:T(1,128)S(1)}, u32[]{:S(2)}, u32[]{:S(2)}) collective-permute-start(f32[6,1,720]{2,1,0:T(1,128)S(1)} %get-tuple-element.46), channel_id=1, source_target_pairs={{0,8},{8,16},{16,24},{24,32},{32,40},{40,48},{48,56},{56,64},{64,7... | collective-permute-start | bytes 51848 | tf_op jit(solution)/shard_map/ppermute | solution.py:17
  338.4 1.9 collective-permute-start.10
  340.8 2.7 collective-permute-done.10
  344.8 4.0 collective-permute-start.13
  348.9 3.2 collective-permute-done.12
  352.8 2.5 fusion.20
  355.5 1.6 fusion.72
  357.2 78.0 %all-reduce.6.cloned.1.call-done = f32[360,128]{1,0:T(8,128)} async-done(((f32[360,128]{1,0:T(8,128)}), f32[360,128]{1,0:T(8,128)}) %all-reduce.6.cloned.1.call-update) | async-done | bytes 184336 | tf_op jit(solution)/shard_map/psum | solution.py:34
  435.3 9.0 %collective-permute-start.15 = (f32[6,1,720]{2,1,0:T(1,128)S(1)}, f32[6,1,720]{2,1,0:T(1,128)S(1)}, u32[]{:S(2)}, u32[]{:S(2)}) collective-permute-start(f32[6,1,720]{2,1,0:T(1,128)S(1)} %get-tuple-element.40), channel_id=1, source_target_pairs={{0,8},{8,16},{16,24},{24,32},{32,40},{40,48},{48,56},{56,64},{64,7... | collective-permute-start | bytes 51848 | tf_op jit(solution)/shard_map/ppermute | solution.py:17
  444.3 1.9 collective-permute-start.14
  446.7 2.7 collective-permute-done.14
  449.4 1.3 collective-permute-start.16
  450.7 4.2 collective-permute-start.17
  455.1 5.8 %collective-permute-done.16 = f32[1,66,720]{2,1,0:T(8,128)S(1)} collective-permute-done((f32[1,66,720]{2,1,0:T(8,128)S(1)}, f32[1,66,720]{2,1,0:T(8,128)S(1)}, u32[]{:S(2)}, u32[]{:S(2)}) %collective-permute-start.16) | collective-permute-done | bytes 190112 | tf_op jit(solution)/shard_map/ppermute | solution.py:19
  460.9 3.3 fusion.7
  464.2 45.7 %all-gather.2.cloned.1.call-done = f32[11520,128]{1,0:T(8,128)} async-done(((f32[360,128]{1,0:T(8,128)}), f32[11520,128]{1,0:T(8,128)}) %all-gather.2.cloned.1.call-update) | async-done | bytes 5898256 | tf_op jit(solution)/shard_map/all_gather | solution.py:144
  509.9 3.3 gather_fusion.1
  513.3 7.0 %fusion.76 = f32[90,1,128]{2,1,0:T(1,128)S(1)} fusion(f32[90,128,128]{2,1,0:T(8,128)} %param.23, f32[90,128,1]{1,0,2:T(8,128)S(1)} %select_bitcast_fusion), kind=kOutput, calls=%fused_computation.147 | convolution fusion | flops 17694720 | bytes 5990400 | tf_op jit(solution)/shard_map/ecf,ec->ef/dot_general | solution.py:150
  (143 shorter events, 16.9 us)
Async XLA Ops:
  7.2 126.8 %reduce-scatter.4.cloned.1.call-start = ((), (), s32[]{:S(2)}) async-start(), calls=%async_computation.4 | async-start | bytes 6082560
  27.9 181.4 %all-reduce.4.cloned.1.call-start = ((), (), s32[]{:S(2)}) async-start(), calls=%async_computation.1 | async-start | bytes 368640 | tf_op jit(solution)/shard_map/psum | solution.py:114
  29.6 18.2 %collective-permute-start.1 = (f32[6,1,720]{2,1,0:T(1,128)}, f32[6,1,720]{2,1,0:T(1,128)}, u32[]{:S(2)}, u32[]{:S(2)}) collective-permute-start(f32[6,1,720]{2,1,0:T(1,128)} %get-tuple-element.58), channel_id=1, source_target_pairs={{0,8},{8,16},{16,24},{24,32},{32,40},{40,48},{48,56},{56,64},{64,7... | collective-permute-start | bytes 51848 | tf_op jit(solution)/shard_map/ppermute | solution.py:17
  34.2 13.7 %collective-permute-start.2 = (f32[6,1,720]{2,1,0:T(1,128)}, f32[6,1,720]{2,1,0:T(1,128)}, u32[]{:S(2)}, u32[]{:S(2)}) collective-permute-start(f32[6,1,720]{2,1,0:T(1,128)} %get-tuple-element.59), channel_id=1, source_target_pairs={{8,0},{16,8},{24,16},{32,24},{40,32},{48,40},{56,48},{64,56},{72,6... | collective-permute-start | bytes 51848 | tf_op jit(solution)/shard_map/ppermute | solution.py:19
  36.8 200.3 %copy-start.3 = (f32[6,64,720]{2,1,0:T(8,128)}, f32[6,64,720]{2,1,0:T(8,128)S(1)}, u32[]{:S(2)}) copy-start(f32[6,64,720]{2,1,0:T(8,128)S(1)} %broadcast_select_fusion.1) | copy-start | bytes 3317764
  36.9 20.3 %collective-permute-start = (f32[6,720]{1,0:T(8,128)S(1)}, f32[6,720]{1,0:T(8,128)S(1)}, u32[]{:S(2)}, u32[]{:S(2)}) collective-permute-start(f32[6,720]{1,0:T(8,128)S(1)} %bitcast.56), channel_id=1, source_target_pairs={{0,8},{8,16},{16,24},{24,32},{32,40},{40,48},{48,56},{56,64},{64,7... | collective-permute-start | bytes 51848 | tf_op jit(solution)/shard_map/ppermute | solution.py:29
  41.1 92.9 %collective-permute-start.4 = (f32[64,720]{1,0:T(8,128)}, f32[64,720]{1,0:T(8,128)S(1)}, u32[]{:S(2)}, u32[]{:S(2)}) collective-permute-start(f32[64,720]{1,0:T(8,128)} %slice_bitcast_fusion), channel_id=1, source_target_pairs={{0,1},{1,2},{2,3},{3,4},{4,5},{5,6},{6,7},{8,9},{9,10},{10,11},{11... | collective-permute-start | bytes 552968 | tf_op jit(solution)/shard_map/ppermute | solution.py:29
  48.7 85.4 %collective-permute-start.3 = (f32[1,66,720]{2,1,0:T(8,128)S(1)}, f32[1,66,720]{2,1,0:T(8,128)S(1)}, u32[]{:S(2)}, u32[]{:S(2)}) collective-permute-start(f32[1,66,720]{2,1,0:T(8,128)S(1)} %get-tuple-element.34), channel_id=1, source_target_pairs={{1,0},{2,1},{3,2},{4,3},{5,4},{6,5},{7,6},{9,8},{10,9},{11,10},{12... | collective-permute-start | bytes 570248 | tf_op jit(solution)/shard_map/ppermute | solution.py:19
  50.1 84.0 %collective-permute-start.5 = (f32[1,66,720]{2,1,0:T(8,128)S(1)}, f32[1,66,720]{2,1,0:T(8,128)S(1)}, u32[]{:S(2)}, u32[]{:S(2)}) collective-permute-start(f32[1,66,720]{2,1,0:T(8,128)S(1)} %get-tuple-element.35), channel_id=1, source_target_pairs={{0,1},{1,2},{2,3},{3,4},{4,5},{5,6},{6,7},{8,9},{9,10},{10,11},{11... | collective-permute-start | bytes 570248 | tf_op jit(solution)/shard_map/ppermute | solution.py:17
  134.0 301.2 %all-reduce.6.cloned.1.call-start = ((), (), s32[]{:S(2)}) async-start(), calls=%async_computation.2 | async-start | bytes 368640 | tf_op jit(solution)/shard_map/psum | solution.py:34
  213.7 11.4 %collective-permute-start.6 = (f32[6,1,720]{2,1,0:T(1,128)S(1)}, f32[6,1,720]{2,1,0:T(1,128)S(1)}, u32[]{:S(2)}, u32[]{:S(2)}) collective-permute-start(f32[6,1,720]{2,1,0:T(1,128)S(1)} %get-tuple-element.52), channel_id=1, source_target_pairs={{0,8},{8,16},{16,24},{24,32},{32,40},{40,48},{48,56},{56,64},{64,7... | collective-permute-start | bytes 51848 | tf_op jit(solution)/shard_map/ppermute | solution.py:17
  222.7 5.1 collective-permute-start.7
  224.6 12.5 %copy-start.14 = (f32[5,64,720]{2,1,0:T(8,128)S(1)}, f32[5,64,720]{2,1,0:T(8,128)}, u32[]{:S(2)}) copy-start(f32[5,64,720]{2,1,0:T(8,128)} %slice.302) | copy-start | bytes 2764804
  224.6 12.5 %copy-start.18 = (f32[6,64,1]{2,1,0:T(8,128)S(1)}, f32[6,64,1]{2,1,0:T(8,128)}, u32[]{:S(2)}) copy-start(f32[6,64,1]{2,1,0:T(8,128)} %slice.242) | copy-start | bytes 4612
  224.6 12.5 %copy-start.22 = (f32[64,720]{1,0:T(8,128)S(1)}, f32[64,720]{1,0:T(8,128)}, u32[]{:S(2)}) copy-start(f32[64,720]{1,0:T(8,128)} %copy-done.21) | copy-start | bytes 552964
  225.0 12.1 %copy-start.7 = (f32[6,64,720]{2,1,0:T(8,128)S(1)}, f32[6,64,720]{2,1,0:T(8,128)}, u32[]{:S(2)}) copy-start(f32[6,64,720]{2,1,0:T(8,128)} %param.21) | copy-start | bytes 3317764
  225.1 12.1 %copy-start.11 = (f32[6,64,720]{2,1,0:T(8,128)S(1)}, f32[6,64,720]{2,1,0:T(8,128)}, u32[]{:S(2)}) copy-start(f32[6,64,720]{2,1,0:T(8,128)} %param.19) | copy-start | bytes 3317764
  225.1 12.1 %copy-start.26 = (f32[6,1,720]{2,1,0:T(1,128)S(1)}, f32[6,1,720]{2,1,0:T(1,128)}, u32[]{:S(2)}) copy-start(f32[6,1,720]{2,1,0:T(1,128)} %broadcast_in_dim.88) | copy-start | bytes 51844
  227.8 9.0 %collective-permute-start.8 = (f32[1,66,720]{2,1,0:T(8,128)S(1)}, f32[1,66,720]{2,1,0:T(8,128)S(1)}, u32[]{:S(2)}, u32[]{:S(2)}) collective-permute-start(f32[1,66,720]{2,1,0:T(8,128)S(1)} %get-tuple-element.32), channel_id=1, source_target_pairs={{1,0},{2,1},{3,2},{4,3},{5,4},{6,5},{7,6},{9,8},{10,9},{11,10},{12... | collective-permute-start | bytes 570248 | tf_op jit(solution)/shard_map/ppermute | solution.py:19
  229.1 8.0 %collective-permute-start.9 = (f32[1,66,720]{2,1,0:T(8,128)S(1)}, f32[1,66,720]{2,1,0:T(8,128)S(1)}, u32[]{:S(2)}, u32[]{:S(2)}) collective-permute-start(f32[1,66,720]{2,1,0:T(8,128)S(1)} %get-tuple-element.33), channel_id=1, source_target_pairs={{0,1},{1,2},{2,3},{3,4},{4,5},{5,6},{6,7},{8,9},{9,10},{10,11},{11... | collective-permute-start | bytes 570248 | tf_op jit(solution)/shard_map/ppermute | solution.py:17
  254.3 13.6 %copy-start.34 = (pred[2048]{0:T(1024)(128)(4,1)S(1)}, pred[2048]{0:T(1024)(128)(4,1)}, u32[]{:S(2)}) copy-start(pred[2048]{0:T(1024)(128)(4,1)} %compare_and_fusion) | copy-start | bytes 6148
  254.3 13.6 %copy-start.38 = (s32[2048]{0:T(1024)S(1)}, s32[2048]{0:T(1024)}, u32[]{:S(2)}) copy-start(s32[2048]{0:T(1024)} %param.29) | copy-start | bytes 24580
  254.3 13.6 %copy-start.39 = (f32[64,6]{0,1:T(8,128)S(1)}, f32[64,6]{0,1:T(8,128)}, u32[]{:S(2)}) copy-start(f32[64,6]{0,1:T(8,128)} %param.26) | copy-start | bytes 4612
  254.3 30.5 %copy-start.32 = (f32[2048]{0:T(1024)S(1)}, f32[2048]{0:T(1024)}, u32[]{:S(2)}) copy-start(f32[2048]{0:T(1024)} %param.31) | copy-start | bytes 24580
  254.3 30.5 %copy-start.33 = (f32[2048]{0:T(1024)S(1)}, f32[2048]{0:T(1024)}, u32[]{:S(2)}) copy-start(f32[2048]{0:T(1024)} %param.30) | copy-start | bytes 24580
  331.1 9.6 %collective-permute-start.11 = (f32[6,1,720]{2,1,0:T(1,128)S(1)}, f32[6,1,720]{2,1,0:T(1,128)S(1)}, u32[]{:S(2)}, u32[]{:S(2)}) collective-permute-start(f32[6,1,720]{2,1,0:T(1,128)S(1)} %get-tuple-element.46), channel_id=1, source_target_pairs={{0,8},{8,16},{16,24},{24,32},{32,40},{40,48},{48,56},{56,64},{64,7... | collective-permute-start | bytes 51848 | tf_op jit(solution)/shard_map/ppermute | solution.py:17
  338.4 5.1 collective-permute-start.10
  340.3 12.5 %copy-start.12 = (f32[6,64,720]{2,1,0:T(8,128)S(1)}, f32[6,64,720]{2,1,0:T(8,128)}, u32[]{:S(2)}) copy-start(f32[6,64,720]{2,1,0:T(8,128)} %param.19) | copy-start | bytes 3317764
  340.3 12.5 %copy-start.15 = (f32[5,64,720]{2,1,0:T(8,128)S(1)}, f32[5,64,720]{2,1,0:T(8,128)}, u32[]{:S(2)}) copy-start(f32[5,64,720]{2,1,0:T(8,128)} %slice.302) | copy-start | bytes 2764804
  340.3 12.5 %copy-start.19 = (f32[6,64,1]{2,1,0:T(8,128)S(1)}, f32[6,64,1]{2,1,0:T(8,128)}, u32[]{:S(2)}) copy-start(f32[6,64,1]{2,1,0:T(8,128)} %slice.242) | copy-start | bytes 4612
  340.3 12.5 %copy-start.23 = (f32[64,720]{1,0:T(8,128)S(1)}, f32[64,720]{1,0:T(8,128)}, u32[]{:S(2)}) copy-start(f32[64,720]{1,0:T(8,128)} %copy-done.21) | copy-start | bytes 552964
  343.5 8.6 %collective-permute-start.12 = (f32[1,66,720]{2,1,0:T(8,128)S(1)}, f32[1,66,720]{2,1,0:T(8,128)S(1)}, u32[]{:S(2)}, u32[]{:S(2)}) collective-permute-start(f32[1,66,720]{2,1,0:T(8,128)S(1)} %get-tuple-element.30), channel_id=1, source_target_pairs={{1,0},{2,1},{3,2},{4,3},{5,4},{6,5},{7,6},{9,8},{10,9},{11,10},{12... | collective-permute-start | bytes 570248 | tf_op jit(solution)/shard_map/ppermute | solution.py:19
  344.8 8.0 %collective-permute-start.13 = (f32[1,66,720]{2,1,0:T(8,128)S(1)}, f32[1,66,720]{2,1,0:T(8,128)S(1)}, u32[]{:S(2)}, u32[]{:S(2)}) collective-permute-start(f32[1,66,720]{2,1,0:T(8,128)S(1)} %get-tuple-element.31), channel_id=1, source_target_pairs={{0,1},{1,2},{2,3},{3,4},{4,5},{5,6},{6,7},{8,9},{9,10},{10,11},{11... | collective-permute-start | bytes 570248 | tf_op jit(solution)/shard_map/ppermute | solution.py:17
  355.3 79.9 %copy-start.35 = (s32[90]{0:T(128)S(1)}, s32[90]{0:T(128)}, u32[]{:S(2)}) copy-start(s32[90]{0:T(128)} %get-tuple-element.65) | copy-start | bytes 1084
  355.3 80.0 %copy-start.36 = (s32[90]{0:T(128)S(1)}, s32[90]{0:T(128)}, u32[]{:S(2)}) copy-start(s32[90]{0:T(128)} %param.25) | copy-start | bytes 1084
  355.3 80.0 %copy-start.37 = (s32[90,1]{0,1:T(1,128)S(1)}, s32[90,1]{0,1:T(1,128)}, u32[]{:S(2)}) copy-start(s32[90,1]{0,1:T(1,128)} %param.24) | copy-start | bytes 1084
  357.2 152.7 %all-gather.2.cloned.1.call-start = ((), (), s32[]{:S(2)}) async-start(), calls=%async_computation.3 | async-start | bytes 6082560 | tf_op jit(solution)/shard_map/all_gather | solution.py:144
  435.3 11.4 %collective-permute-start.15 = (f32[6,1,720]{2,1,0:T(1,128)S(1)}, f32[6,1,720]{2,1,0:T(1,128)S(1)}, u32[]{:S(2)}, u32[]{:S(2)}) collective-permute-start(f32[6,1,720]{2,1,0:T(1,128)S(1)} %get-tuple-element.40), channel_id=1, source_target_pairs={{0,8},{8,16},{16,24},{24,32},{32,40},{40,48},{48,56},{56,64},{64,7... | collective-permute-start | bytes 51848 | tf_op jit(solution)/shard_map/ppermute | solution.py:17
  444.3 5.1 collective-permute-start.14
  446.2 14.6 %copy-start.13 = (f32[6,64,720]{2,1,0:T(8,128)S(1)}, f32[6,64,720]{2,1,0:T(8,128)}, u32[]{:S(2)}) copy-start(f32[6,64,720]{2,1,0:T(8,128)} %param.19) | copy-start | bytes 3317764
  446.3 14.6 %copy-start.16 = (f32[5,64,720]{2,1,0:T(8,128)S(1)}, f32[5,64,720]{2,1,0:T(8,128)}, u32[]{:S(2)}) copy-start(f32[5,64,720]{2,1,0:T(8,128)} %slice.302) | copy-start | bytes 2764804
  446.3 14.6 %copy-start.20 = (f32[6,64,1]{2,1,0:T(8,128)S(1)}, f32[6,64,1]{2,1,0:T(8,128)}, u32[]{:S(2)}) copy-start(f32[6,64,1]{2,1,0:T(8,128)} %slice.242) | copy-start | bytes 4612
  446.3 14.6 %copy-start.24 = (f32[64,720]{1,0:T(8,128)S(1)}, f32[64,720]{1,0:T(8,128)}, u32[]{:S(2)}) copy-start(f32[64,720]{1,0:T(8,128)} %copy-done.21) | copy-start | bytes 552964
  446.7 14.2 %copy-start.5 = (f32[6,64,720]{2,1,0:T(8,128)S(1)}, f32[6,64,720]{2,1,0:T(8,128)}, u32[]{:S(2)}) copy-start(f32[6,64,720]{2,1,0:T(8,128)} %copy-done.3) | copy-start | bytes 3317764
  446.7 14.2 %copy-start.9 = (f32[6,64,720]{2,1,0:T(8,128)S(1)}, f32[6,64,720]{2,1,0:T(8,128)}, u32[]{:S(2)}) copy-start(f32[6,64,720]{2,1,0:T(8,128)} %param.21) | copy-start | bytes 3317764
  446.7 14.2 %copy-start.28 = (f32[6,1,720]{2,1,0:T(1,128)S(1)}, f32[6,1,720]{2,1,0:T(1,128)}, u32[]{:S(2)}) copy-start(f32[6,1,720]{2,1,0:T(1,128)} %broadcast_in_dim.88) | copy-start | bytes 51844
  449.4 11.4 %collective-permute-start.16 = (f32[1,66,720]{2,1,0:T(8,128)S(1)}, f32[1,66,720]{2,1,0:T(8,128)S(1)}, u32[]{:S(2)}, u32[]{:S(2)}) collective-permute-start(f32[1,66,720]{2,1,0:T(8,128)S(1)} %get-tuple-element.28), channel_id=1, source_target_pairs={{1,0},{2,1},{3,2},{4,3},{5,4},{6,5},{7,6},{9,8},{10,9},{11,10},{12... | collective-permute-start | bytes 570248 | tf_op jit(solution)/shard_map/ppermute | solution.py:19
  450.7 10.1 %collective-permute-start.17 = (f32[1,66,720]{2,1,0:T(8,128)S(1)}, f32[1,66,720]{2,1,0:T(8,128)S(1)}, u32[]{:S(2)}, u32[]{:S(2)}) collective-permute-start(f32[1,66,720]{2,1,0:T(8,128)S(1)} %get-tuple-element.29), channel_id=1, source_target_pairs={{0,1},{1,2},{2,3},{3,4},{4,5},{5,6},{6,7},{8,9},{9,10},{10,11},{11... | collective-permute-start | bytes 570248 | tf_op jit(solution)/shard_map/ppermute | solution.py:17
  (14 other events, 77.2 us)
Sparse Core Ops, SparseCore 0:
  28.0 105.9 reduce-scatter.3
  136.6 72.6 all-reduce.3
  357.3 77.8 all-reduce.5
  437.7 72.1 all-gather.1
where the time goes:
time: 529 us; the launch traced here: 527 us
  waiting for transfers between devices  289 us (55%)
  local copies, waits for them, and re-layouts  70.2 us (13%)
  starting transfers between devices  66.4 us (13%)
  other arithmetic  51.3 us (10%)
  matrix products  19.1 us (4%)
  blocking collectives  15.9 us (3%)
  between operations  15.3 us (3%)
    psum x1, waiting for transfers between devices, spread(): return lax.psum(block, axis)  78 us
    unnamed x5, waiting for transfers between devices  76.2 us
    psum x1, waiting for transfers between devices, on_device(): surface = lax.psum(partial_value, 'lev').reshape(rows, cols)  67.9 us
    ppermute x8, starting transfers between devices, with_halo(): lax.ppermute(tail, axis, [(i, (i + 1) % count) for i in range(ends)])  46 us
    all_gather x1, waiting for transfers between devices, on_device(): piece = lax.all_gather(shared, 'tile', axis=0, tiled=True)  45.7 us
    scatter-add x1, other arithmetic, on_device(): adjoint_two = jnp.zeros((levels, rows * cols), jnp.float32).at[:, sound_c...  20.8 us
    ppermute x8, waiting for transfers between devices, with_halo(): lax.ppermute(head, axis, [((i + 1) % count, i) for i in range(ends)])  20.6 us
    psum x1, blocking collectives, on_device(): column = lax.psum(partial_column, 'lev')  15.9 us
  transfers between devices with their start and end apart: 22, of which 12 were waited for; matrix products, arithmetic and copies ran while one was open for 4% of the time, Pallas kernels for 0%

commit v1 on v0

--- a/solution.py
+++ b/solution.py
@@ -141,7 +141,10 @@
     adjoint_one = transport(adjoint_two, coeffs, True)
     surface_bar = (adjoint_two[0] + adjoint_one[0]).reshape(blocks, block_size)
     shared = spread(surface_bar, "lev", 0)
-    piece = lax.all_gather(shared, "tile", axis=0, tiled=True)
+    size = lax.axis_size("tile")
+    pieces = jnp.stack([shared for _ in range(size)])
+    pieces = lax.all_to_all(pieces, "tile", split_axis=0, concat_axis=0)
+    piece = jnp.concatenate(pieces, axis=0)
     local = global_rows
     inside = (local >= 0) & (local < piece.shape[0])
     found = piece[jnp.clip(local, 0, piece.shape[0] - 1)]

time: 529 us -> 652 us (1.23)
  the two profiles are of different devices: /device:TPU:1 before, /device:TPU:66 now
where the time goes in v1:
time: 652 us; the launch traced here: 643 us
  waiting for transfers between devices  358 us (55%)
  local copies, waits for them, and re-layouts  96.3 us (15%)
  starting transfers between devices  71.9 us (11%)
  other arithmetic  67.5 us (10%)
  matrix products  19.1 us (3%)
  between operations  15.6 us (2%)
  blocking collectives  14.2 us (2%)
    ppermute x8, waiting for transfers between devices, with_halo(): lax.ppermute(tail, axis, [(i, (i + 1) % count) for i in range(ends)])  137 us
    psum x1, waiting for transfers between devices, spread(): return lax.psum(block, axis)  75.9 us
    unnamed x4, waiting for transfers between devices  68.1 us
    psum x1, waiting for transfers between devices, on_device(): surface = lax.psum(partial_value, 'lev').reshape(rows, cols)  67.8 us
    ppermute x8, starting transfers between devices, with_halo(): lax.ppermute(head, axis, [((i + 1) % count, i) for i in range(ends)])  36.1 us
    add x4, other arithmetic, apply_step(): return field + rows_term + cols_term + diffusion  32.7 us
    scatter-add x3, local copies, waits for them, and re-layouts, on_device(): state = state.at[0].add(emission)  23.5 us
    scatter-add x1, other arithmetic, on_device(): adjoint_two = jnp.zeros((levels, rows * cols), jnp.float32).at[:, sound_c...  20.7 us
  transfers between devices with their start and end apart: 22, of which 12 were waited for; matrix products, arithmetic and copies ran while one was open for 6% of the time, Pallas kernels for 0%

profile of v1, /device:TPU:66, one launch (start us, length us, event | category | flops | bytes accessed | tf_op | source)
XLA Modules:
  0.0 643.0 jit_solution(6239250808441660258)
XLA Ops:
  7.9 11.2 %fusion.92 = f32[90,1,128]{2,1,0:T(1,128)S(1)} fusion(f32[90,128,128]{2,1,0:T(8,128)} %param.23, f32[90,128,1]{1,2,0:T(1,128)S(1)} %bitcast.53), kind=kOutput, calls=%fused_computation.176 | convolution fusion | flops 17694720 | bytes 5990400 | tf_op jit(solution)/shard_map/ecf,ef->ec/dot_general | solution.py:103
  19.1 3.8 scatter_custom_fusion
  22.9 4.5 slice.314
  27.5 2.1 copy.131
  29.5 3.5 collective-permute-start.2
  33.0 1.9 collective-permute-start.1
  36.9 2.0 collective-permute-start
  39.0 2.1 copy_select_fusion
  42.3 3.8 collective-permute-start.4
  47.0 2.2 fusion.89
  52.2 3.0 collective-permute-start.3
  55.2 2.9 collective-permute-start.5
  64.1 68.1 %reduce-scatter.4.cloned.1.call-done = f32[360,128]{1,0:T(8,128)} async-done(((f32[11520,128]{1,0:T(8,128)}), f32[360,128]{1,0:T(8,128)}) %reduce-scatter.4.cloned.1.call-update) | async-done | bytes 184336
  132.7 10.5 %fusion.46 = f32[6,64,720]{2,0,1:T(8,128)S(1)} fusion(f32[6,64,720]{2,0,1:T(8,128)} %copy-done.15, f32[6,66,720]{2,0,1:T(8,128)} %copy-done.30, f32[1,66,720]{2,0,1:T(1,128)} %collective-permute-done.5, f32[1,66,720]{2,0,1:T(1,128)} %collective-permute-done.3, f32[6,1,720]{2,0,1:T(8,128)S(1)} %collective-permute-done.2, ...), kind=kLoop, calls=%fused_computation.76 | loop fusion | flops 11335680 | bytes 12614470 | tf_op jit(solution)/shard_map/add | solution.py:56
  143.2 67.8 %all-reduce.4.cloned.1.call-done = f32[360,128]{1,0:T(8,128)} async-done(((f32[360,128]{1,0:T(8,128)}), f32[360,128]{1,0:T(8,128)}) %all-reduce.4.cloned.1.call-update) | async-done | bytes 184336 | tf_op jit(solution)/shard_map/psum | solution.py:114
  215.6 6.5 %scatter-add.25 = f32[6,64,720]{2,0,1:T(8,128)S(1)} dynamic-update-slice(f32[6,64,720]{2,0,1:T(8,128)S(1)} %fusion.46, f32[1,64,720]{2,0,1:T(1,128)} %slice_add_fusion.1, s32[]{:T(128)} %constant.86.clone.1, s32[]{:T(128)} %constant.86.clone.1, s32[]{:T(128)} %constant.86.clone.1) | dynamic-update-slice | bytes 368644 | tf_op jit(solution)/shard_map/scatter-add | solution.py:116
  222.1 1.9 collective-permute-start.6
  224.0 6.7 %collective-permute-start.7 = (f32[6,1,720]{2,0,1:T(8,128)S(1)}, f32[6,1,720]{2,0,1:T(8,128)S(1)}, u32[]{:S(2)}, u32[]{:S(2)}) collective-permute-start(f32[6,1,720]{2,0,1:T(8,128)S(1)} %get-tuple-element.65), channel_id=1, source_target_pairs={{8,0},{16,8},{24,16},{32,24},{40,32},{48,40},{56,48},{64,56},{72,6... | collective-permute-start | bytes 51848 | tf_op jit(solution)/shard_map/ppermute | solution.py:19
  232.5 2.5 collective-permute-start.8
  235.0 3.5 collective-permute-start.9
  238.6 3.7 collective-permute-done.8
  242.4 4.5 collective-permute-done.9
  247.0 7.5 %fusion.33 = f32[6,64,720]{2,0,1:T(8,128)S(1)} fusion(f32[6,64,720]{2,0,1:T(8,128)S(1)} %scatter-add.25, f32[1,66,720]{2,0,1:T(1,128)S(1)} %collective-permute-done.9, f32[6,1,720]{2,0,1:T(8,128)S(1)} %collective-permute-done.7, f32[6,1,720]{2,0,1:T(8,128)S(1)} %collective-permute-done.6, f32[1,66,720]{2,0,1:T(1,128)S(1)} %collective-permute-done.8, ...), kind=kLoop, calls=%fused_computation.55 | loop fusion | flops 12441600 | bytes 11473990 | tf_op jit(solution)/shard_map/add | solution.py:56
  255.8 5.0 scatter-add.26
  260.8 12.0 %copy.147 = f32[6,64,720]{0,2,1:T(8,128)} copy(f32[6,64,720]{2,0,1:T(8,128)} %scatter-add.26) | data formatting | bytes 2211840 | tf_op jit(solution)/shard_map/scatter-add | solution.py:118
  272.8 13.2 %gather_fusion = f32[2048,6]{1,0:T(8,128)S(1)} fusion(f32[6,46080]{0,1:T(8,128)} %bitcast.47, s32[2048]{0:T(1024)S(1)} %get-tuple-element.76), kind=kCustom, calls=%fused_computation | custom fusion | bytes 106496 | tf_op jit(solution)/shard_map/jit(_take)/gather | solution.py:126
  287.4 14.2 %psum.22 = f32[2048]{0:T(1024)S(1)} all-reduce(f32[2048]{0:T(1024)S(1)} %get-tuple-element.79), channel_id=1, replica_groups=mesh['tile'=32,'lev'=8] {'lev'}, use_global_device_ids=true, to_apply=%region_4.5 | all-reduce | flops 2048 | bytes 16384 | tf_op jit(solution)/shard_map/psum | solution.py:128
  302.7 20.7 %scatter_custom_fusion.1 = f32[6,46080]{0,1:T(8,128)} fusion(s32[2048]{0:T(1024)S(1)} %get-tuple-element.75, f32[2048,6]{1,0:T(8,128)S(1)} %copy.149, f32[]{:T(128)} %constant.93.clone.1), kind=kCustom, calls=%fused_computation.5 | custom fusion | flops 12288 | bytes 1105924 | tf_op jit(solution)/shard_map/scatter-add | solution.py:138
  323.4 11.9 %slice_reduce_fusion = f32[46080]{0:T(1024)} fusion(f32[6,46080]{0,1:T(8,128)} %scatter_custom_fusion.1), kind=kLoop, calls=%fused_computation.4 | loop fusion | bytes 368640 | tf_op jit(solution)/shard_map/slice | solution.py:142
  335.3 12.5 %copy.156 = f32[6,64,720]{2,0,1:T(8,128)S(1)} copy(f32[6,64,720]{0,2,1:T(8,128)} %bitcast.41) | data formatting | bytes 2211840 | tf_op jit(solution)/shard_map/reshape | solution.py:140
  347.8 1.9 collective-permute-start.11
  349.8 6.7 %collective-permute-start.10 = (f32[6,1,720]{2,0,1:T(8,128)S(1)}, f32[6,1,720]{2,0,1:T(8,128)S(1)}, u32[]{:S(2)}, u32[]{:S(2)}) collective-permute-start(f32[6,1,720]{2,0,1:T(8,128)S(1)} %get-tuple-element.59), channel_id=1, source_target_pairs={{8,0},{16,8},{24,16},{32,24},{40,32},{48,40},{56,48},{64,56},{72,6... | collective-permute-start | bytes 51848 | tf_op jit(solution)/shard_map/ppermute | solution.py:19
  358.2 5.2 collective-permute-start.12
  363.4 1.9 collective-permute-start.13
  365.5 2.1 collective-permute-done.12
  367.5 5.0 collective-permute-done.13
  372.6 7.3 %fusion.20 = f32[6,64,720]{2,0,1:T(8,128)S(1)} fusion(f32[6,64,720]{2,0,1:T(8,128)S(1)} %copy.156, f32[1,66,720]{2,0,1:T(1,128)S(1)} %collective-permute-done.13, f32[6,1,720]{2,0,1:T(8,128)S(1)} %collective-permute-done.10, f32[6,1,720]{2,0,1:T(8,128)S(1)} %collective-permute-done.11, f32[1,66,720]{2,0,1:T(1,128)S(1)} %collective-permute-done.12, ...), kind=kLoop, calls=%fused_computation.34 | loop fusion | flops 10229760 | bytes 11473990 | tf_op jit(solution)/shard_map/add | solution.py:56
  382.3 75.9 %all-reduce.6.cloned.1.call-done = f32[360,128]{1,0:T(8,128)} async-done(((f32[360,128]{1,0:T(8,128)}), f32[360,128]{1,0:T(8,128)}) %all-reduce.6.cloned.1.call-update) | async-done | bytes 184336 | tf_op jit(solution)/shard_map/psum | solution.py:34
  458.2 3.8 stack.2
  462.0 9.3 %all-to-all-start = ((f32[32,360,128]{2,1,0:T(8,128)}), f32[32,360,128]{2,1,0:T(8,128)}, u32[]{:S(2)}, u32[]{:S(2)}) async-start(f32[32,360,128]{2,1,0:T(8,128)} %stack.2), calls=%async_computation | async-start | bytes 11796480 | tf_op jit(solution)/shard_map/all_to_all | solution.py:146
  471.4 2.0 collective-permute-start.15
  473.4 6.8 %collective-permute-start.14 = (f32[6,1,720]{2,0,1:T(8,128)S(1)}, f32[6,1,720]{2,0,1:T(8,128)S(1)}, u32[]{:S(2)}, u32[]{:S(2)}) collective-permute-start(f32[6,1,720]{2,0,1:T(8,128)S(1)} %get-tuple-element.53), channel_id=1, source_target_pairs={{8,0},{16,8},{24,16},{32,24},{40,32},{48,40},{56,48},{64,56},{72,6... | collective-permute-start | bytes 51848 | tf_op jit(solution)/shard_map/ppermute | solution.py:19
  480.8 124.8 %collective-permute-done.15 = f32[6,1,720]{2,0,1:T(8,128)S(1)} collective-permute-done((f32[6,1,720]{2,0,1:T(8,128)S(1)}, f32[6,1,720]{2,0,1:T(8,128)S(1)}, u32[]{:S(2)}, u32[]{:S(2)}) %collective-permute-start.15) | collective-permute-done | bytes 17312 | tf_op jit(solution)/shard_map/ppermute | solution.py:17
  607.9 3.9 collective-permute-start.17
  613.6 2.8 collective-permute-done.17
  616.5 7.3 %fusion.7 = f32[6,64,720]{2,0,1:T(8,128)S(1)} fusion(f32[6,64,720]{2,0,1:T(8,128)S(1)} %fusion.20, f32[1,66,720]{2,0,1:T(1,128)S(1)} %collective-permute-done.17, f32[6,1,720]{2,0,1:T(8,128)S(1)} %collective-permute-done.14, f32[6,1,720]{2,0,1:T(8,128)S(1)} %collective-permute-done.15, f32[1,66,720]{2,0,1:T(1,128)S(1)} %collective-permute-done.16, ...), kind=kLoop, calls=%fused_computation.13 | loop fusion | flops 10229760 | bytes 11473990 | tf_op jit(solution)/shard_map/add | solution.py:56
  625.2 3.3 gather_fusion.1
  628.6 7.0 %fusion.74 = f32[90,1,128]{2,1,0:T(1,128)S(1)} fusion(f32[90,128,128]{2,1,0:T(8,128)} %param.23, f32[90,128,1]{1,0,2:T(8,128)S(1)} %select_bitcast_fusion), kind=kOutput, calls=%fused_computation.140 | convolution fusion | flops 17694720 | bytes 5990400 | tf_op jit(solution)/shard_map/ecf,ec->ef/dot_general | solution.py:153
  (150 shorter events, 34.5 us)
Async XLA Ops:
  7.2 125.0 %reduce-scatter.4.cloned.1.call-start = ((), (), s32[]{:S(2)}) async-start(), calls=%async_computation.4 | async-start | bytes 6082560
  27.4 183.7 %all-reduce.4.cloned.1.call-start = ((), (), s32[]{:S(2)}) async-start(), calls=%async_computation.2 | async-start | bytes 368640 | tf_op jit(solution)/shard_map/psum | solution.py:114
  29.5 17.5 %copy-start.15 = (f32[6,64,720]{2,0,1:T(8,128)}, f32[6,64,720]{2,0,1:T(8,128)S(1)}, u32[]{:S(2)}) copy-start(f32[6,64,720]{2,0,1:T(8,128)S(1)} %copy.131) | copy-start | bytes 3317764
  29.5 20.4 %collective-permute-start.2 = (f32[6,1,720]{2,0,1:T(8,128)S(1)}, f32[6,1,720]{2,0,1:T(8,128)S(1)}, u32[]{:S(2)}, u32[]{:S(2)}) collective-permute-start(f32[6,1,720]{2,0,1:T(8,128)S(1)} %get-tuple-element.70), channel_id=1, source_target_pairs={{8,0},{16,8},{24,16},{32,24},{40,32},{48,40},{56,48},{64,56},{72,6... | collective-permute-start | bytes 51848 | tf_op jit(solution)/shard_map/ppermute | solution.py:19
  33.0 16.2 %collective-permute-start.1 = (f32[6,1,720]{2,0,1:T(8,128)S(1)}, f32[6,1,720]{2,0,1:T(8,128)S(1)}, u32[]{:S(2)}, u32[]{:S(2)}) collective-permute-start(f32[6,1,720]{2,0,1:T(8,128)S(1)} %get-tuple-element.71), channel_id=1, source_target_pairs={{0,8},{8,16},{16,24},{24,32},{32,40},{40,48},{48,56},{56,64},{64,7... | collective-permute-start | bytes 51848 | tf_op jit(solution)/shard_map/ppermute | solution.py:17
  36.9 95.8 %collective-permute-start = (f32[6,720]{1,0:T(8,128)S(1)}, f32[6,720]{1,0:T(8,128)S(1)}, u32[]{:S(2)}, u32[]{:S(2)}) collective-permute-start(f32[6,720]{1,0:T(8,128)S(1)} %slice_bitcast_fusion), channel_id=1, source_target_pairs={{0,8},{8,16},{16,24},{24,32},{32,40},{40,48},{48,56},{56,64},{64,7... | collective-permute-start | bytes 51848 | tf_op jit(solution)/shard_map/ppermute | solution.py:29
  41.1 205.8 %copy-start.2 = (f32[6,64,720]{2,0,1:T(8,128)}, f32[6,64,720]{2,0,1:T(8,128)S(1)}, u32[]{:S(2)}) copy-start(f32[6,64,720]{2,0,1:T(8,128)S(1)} %copy_select_fusion) | copy-start | bytes 3317764
  42.3 20.1 %collective-permute-start.4 = (f32[64,720]{1,0:T(8,128)}, f32[64,720]{1,0:T(8,128)}, u32[]{:S(2)}, u32[]{:S(2)}) collective-permute-start(f32[64,720]{1,0:T(8,128)} %bitcast.36), channel_id=1, source_target_pairs={{0,1},{1,2},{2,3},{3,4},{4,5},{5,6},{6,7},{8,9},{9,10},{10,11},{11... | collective-permute-start | bytes 552968 | tf_op jit(solution)/shard_map/ppermute | solution.py:29
  52.2 80.5 %collective-permute-start.3 = (f32[1,66,720]{2,0,1:T(1,128)}, f32[1,66,720]{2,0,1:T(1,128)}, u32[]{:S(2)}, u32[]{:S(2)}) collective-permute-start(f32[1,66,720]{2,0,1:T(1,128)} %get-tuple-element.46), channel_id=1, source_target_pairs={{1,0},{2,1},{3,2},{4,3},{5,4},{6,5},{7,6},{9,8},{10,9},{11,10},{12... | collective-permute-start | bytes 570248 | tf_op jit(solution)/shard_map/ppermute | solution.py:19
  55.2 77.5 %collective-permute-start.5 = (f32[1,66,720]{2,0,1:T(1,128)}, f32[1,66,720]{2,0,1:T(1,128)}, u32[]{:S(2)}, u32[]{:S(2)}) collective-permute-start(f32[1,66,720]{2,0,1:T(1,128)} %get-tuple-element.47), channel_id=1, source_target_pairs={{0,1},{1,2},{2,3},{3,4},{4,5},{5,6},{6,7},{8,9},{9,10},{10,11},{11... | collective-permute-start | bytes 570248 | tf_op jit(solution)/shard_map/ppermute | solution.py:17
  132.2 326.0 %all-reduce.6.cloned.1.call-start = ((), (), s32[]{:S(2)}) async-start(), calls=%async_computation.3 | async-start | bytes 368640 | tf_op jit(solution)/shard_map/psum | solution.py:34
  222.1 9.2 %collective-permute-start.6 = (f32[6,1,720]{2,0,1:T(8,128)S(1)}, f32[6,1,720]{2,0,1:T(8,128)S(1)}, u32[]{:S(2)}, u32[]{:S(2)}) collective-permute-start(f32[6,1,720]{2,0,1:T(8,128)S(1)} %get-tuple-element.64), channel_id=1, source_target_pairs={{0,8},{8,16},{16,24},{24,32},{32,40},{40,48},{48,56},{56,64},{64,7... | collective-permute-start | bytes 51848 | tf_op jit(solution)/shard_map/ppermute | solution.py:17
  224.0 8.2 %collective-permute-start.7 = (f32[6,1,720]{2,0,1:T(8,128)S(1)}, f32[6,1,720]{2,0,1:T(8,128)S(1)}, u32[]{:S(2)}, u32[]{:S(2)}) collective-permute-start(f32[6,1,720]{2,0,1:T(8,128)S(1)} %get-tuple-element.65), channel_id=1, source_target_pairs={{8,0},{16,8},{24,16},{32,24},{40,32},{48,40},{56,48},{64,56},{72,6... | collective-permute-start | bytes 51848 | tf_op jit(solution)/shard_map/ppermute | solution.py:19
  230.7 16.2 %copy-start.8 = (f32[6,63,720]{2,0,1:T(8,128)S(1)}, f32[6,63,720]{2,0,1:T(8,128)}, u32[]{:S(2)}) copy-start(f32[6,63,720]{2,0,1:T(8,128)} %slice.300) | copy-start | bytes 3265924
  230.7 16.2 %copy-start.17 = (f32[6,64,720]{2,1,0:T(8,128)S(1)}, f32[6,64,720]{2,1,0:T(8,128)}, u32[]{:S(2)}) copy-start(f32[6,64,720]{2,1,0:T(8,128)} %param.19) | copy-start | bytes 3317764
  230.7 16.2 %copy-start.20 = (f32[6,64,720]{2,1,0:T(8,128)S(1)}, f32[6,64,720]{2,1,0:T(8,128)}, u32[]{:S(2)}) copy-start(f32[6,64,720]{2,1,0:T(8,128)} %param.21) | copy-start | bytes 3317764
  231.2 15.7 %copy-start.5 = (f32[6,64,719]{2,0,1:T(8,128)S(1)}, f32[6,64,719]{2,0,1:T(8,128)}, u32[]{:S(2)}) copy-start(f32[6,64,719]{2,0,1:T(8,128)} %copy.203) | copy-start | bytes 3313156
  231.3 15.7 %copy-start.12 = (f32[6,64,720]{2,1,0:T(8,128)S(1)}, f32[6,64,720]{2,1,0:T(8,128)}, u32[]{:S(2)}) copy-start(f32[6,64,720]{2,1,0:T(8,128)} %param.20) | copy-start | bytes 3317764
  231.3 15.7 %copy-start.26 = (f32[1,64,720]{2,0,1:T(1,128)S(1)}, f32[1,64,720]{2,0,1:T(1,128)}, u32[]{:S(2)}) copy-start(f32[1,64,720]{2,0,1:T(1,128)} %broadcast_in_dim.90) | copy-start | bytes 552964
  232.5 9.8 %collective-permute-start.8 = (f32[1,66,720]{2,0,1:T(1,128)S(1)}, f32[1,66,720]{2,0,1:T(1,128)S(1)}, u32[]{:S(2)}, u32[]{:S(2)}) collective-permute-start(f32[1,66,720]{2,0,1:T(1,128)S(1)} %get-tuple-element.44), channel_id=1, source_target_pairs={{1,0},{2,1},{3,2},{4,3},{5,4},{6,5},{7,6},{9,8},{10,9},{11,10},{12... | collective-permute-start | bytes 570248 | tf_op jit(solution)/shard_map/ppermute | solution.py:19
  235.0 11.9 %collective-permute-start.9 = (f32[1,66,720]{2,0,1:T(1,128)S(1)}, f32[1,66,720]{2,0,1:T(1,128)S(1)}, u32[]{:S(2)}, u32[]{:S(2)}) collective-permute-start(f32[1,66,720]{2,0,1:T(1,128)S(1)} %get-tuple-element.45), channel_id=1, source_target_pairs={{0,1},{1,2},{2,3},{3,4},{4,5},{5,6},{6,7},{8,9},{9,10},{10,11},{11... | collective-permute-start | bytes 570248 | tf_op jit(solution)/shard_map/ppermute | solution.py:17
  272.8 13.6 %copy-start.37 = (s32[2048]{0:T(1024)S(1)}, s32[2048]{0:T(1024)}, u32[]{:S(2)}) copy-start(s32[2048]{0:T(1024)} %param.29) | copy-start | bytes 24580
  272.8 13.6 %copy-start.38 = (f32[64,6]{0,1:T(8,128)S(1)}, f32[64,6]{0,1:T(8,128)}, u32[]{:S(2)}) copy-start(f32[64,6]{0,1:T(8,128)} %param.26) | copy-start | bytes 4612
  272.8 28.8 %copy-start.33 = (f32[2048]{0:T(1024)S(1)}, f32[2048]{0:T(1024)}, u32[]{:S(2)}) copy-start(f32[2048]{0:T(1024)} %param.31) | copy-start | bytes 24580
  272.8 28.8 %copy-start.34 = (f32[2048]{0:T(1024)S(1)}, f32[2048]{0:T(1024)}, u32[]{:S(2)}) copy-start(f32[2048]{0:T(1024)} %param.30) | copy-start | bytes 24580
  347.8 9.2 %collective-permute-start.11 = (f32[6,1,720]{2,0,1:T(8,128)S(1)}, f32[6,1,720]{2,0,1:T(8,128)S(1)}, u32[]{:S(2)}, u32[]{:S(2)}) collective-permute-start(f32[6,1,720]{2,0,1:T(8,128)S(1)} %get-tuple-element.58), channel_id=1, source_target_pairs={{0,8},{8,16},{16,24},{24,32},{32,40},{40,48},{48,56},{56,64},{64,7... | collective-permute-start | bytes 51848 | tf_op jit(solution)/shard_map/ppermute | solution.py:17
  349.8 8.2 %collective-permute-start.10 = (f32[6,1,720]{2,0,1:T(8,128)S(1)}, f32[6,1,720]{2,0,1:T(8,128)S(1)}, u32[]{:S(2)}, u32[]{:S(2)}) collective-permute-start(f32[6,1,720]{2,0,1:T(8,128)S(1)} %get-tuple-element.59), channel_id=1, source_target_pairs={{8,0},{16,8},{24,16},{32,24},{40,32},{48,40},{56,48},{64,56},{72,6... | collective-permute-start | bytes 51848 | tf_op jit(solution)/shard_map/ppermute | solution.py:19
  356.4 16.1 %copy-start.6 = (f32[6,64,719]{2,0,1:T(8,128)S(1)}, f32[6,64,719]{2,0,1:T(8,128)}, u32[]{:S(2)}) copy-start(f32[6,64,719]{2,0,1:T(8,128)} %copy.203) | copy-start | bytes 3313156
  356.4 16.1 %copy-start.9 = (f32[6,63,720]{2,0,1:T(8,128)S(1)}, f32[6,63,720]{2,0,1:T(8,128)}, u32[]{:S(2)}) copy-start(f32[6,63,720]{2,0,1:T(8,128)} %slice.300) | copy-start | bytes 3265924
  356.4 16.1 %copy-start.18 = (f32[6,64,720]{2,1,0:T(8,128)S(1)}, f32[6,64,720]{2,1,0:T(8,128)}, u32[]{:S(2)}) copy-start(f32[6,64,720]{2,1,0:T(8,128)} %param.19) | copy-start | bytes 3317764
  356.4 16.1 %copy-start.21 = (f32[6,64,720]{2,1,0:T(8,128)S(1)}, f32[6,64,720]{2,1,0:T(8,128)}, u32[]{:S(2)}) copy-start(f32[6,64,720]{2,1,0:T(8,128)} %param.21) | copy-start | bytes 3317764
  357.0 15.6 %copy-start.3 = (f32[6,64,720]{2,0,1:T(8,128)S(1)}, f32[6,64,720]{2,0,1:T(8,128)}, u32[]{:S(2)}) copy-start(f32[6,64,720]{2,0,1:T(8,128)} %copy-done.2) | copy-start | bytes 3317764
  357.0 15.6 %copy-start.13 = (f32[6,64,720]{2,1,0:T(8,128)S(1)}, f32[6,64,720]{2,1,0:T(8,128)}, u32[]{:S(2)}) copy-start(f32[6,64,720]{2,1,0:T(8,128)} %param.20) | copy-start | bytes 3317764
  357.0 15.6 %copy-start.27 = (f32[1,64,720]{2,0,1:T(1,128)S(1)}, f32[1,64,720]{2,0,1:T(1,128)}, u32[]{:S(2)}) copy-start(f32[1,64,720]{2,0,1:T(1,128)} %broadcast_in_dim.90) | copy-start | bytes 552964
  358.2 9.3 %collective-permute-start.12 = (f32[1,66,720]{2,0,1:T(1,128)S(1)}, f32[1,66,720]{2,0,1:T(1,128)S(1)}, u32[]{:S(2)}, u32[]{:S(2)}) collective-permute-start(f32[1,66,720]{2,0,1:T(1,128)S(1)} %get-tuple-element.42), channel_id=1, source_target_pairs={{1,0},{2,1},{3,2},{4,3},{5,4},{6,5},{7,6},{9,8},{10,9},{11,10},{12... | collective-permute-start | bytes 570248 | tf_op jit(solution)/shard_map/ppermute | solution.py:19
  363.4 9.1 %collective-permute-start.13 = (f32[1,66,720]{2,0,1:T(1,128)S(1)}, f32[1,66,720]{2,0,1:T(1,128)S(1)}, u32[]{:S(2)}, u32[]{:S(2)}) collective-permute-start(f32[1,66,720]{2,0,1:T(1,128)S(1)} %get-tuple-element.43), channel_id=1, source_target_pairs={{0,1},{1,2},{2,3},{3,4},{4,5},{5,6},{6,7},{8,9},{9,10},{10,11},{11... | collective-permute-start | bytes 570248 | tf_op jit(solution)/shard_map/ppermute | solution.py:17
  462.0 163.1 %all-to-all-start = ((f32[32,360,128]{2,1,0:T(8,128)}), f32[32,360,128]{2,1,0:T(8,128)}, u32[]{:S(2)}, u32[]{:S(2)}) async-start(f32[32,360,128]{2,1,0:T(8,128)} %stack.2), calls=%async_computation | async-start | bytes 11796480 | tf_op jit(solution)/shard_map/all_to_all | solution.py:146
  471.4 134.2 %collective-permute-start.15 = (f32[6,1,720]{2,0,1:T(8,128)S(1)}, f32[6,1,720]{2,0,1:T(8,128)S(1)}, u32[]{:S(2)}, u32[]{:S(2)}) collective-permute-start(f32[6,1,720]{2,0,1:T(8,128)S(1)} %get-tuple-element.52), channel_id=1, source_target_pairs={{0,8},{8,16},{16,24},{24,32},{32,40},{40,48},{48,56},{56,64},{64,7... | collective-permute-start | bytes 51848 | tf_op jit(solution)/shard_map/ppermute | solution.py:17
  473.4 132.2 %collective-permute-start.14 = (f32[6,1,720]{2,0,1:T(8,128)S(1)}, f32[6,1,720]{2,0,1:T(8,128)S(1)}, u32[]{:S(2)}, u32[]{:S(2)}) collective-permute-start(f32[6,1,720]{2,0,1:T(8,128)S(1)} %get-tuple-element.53), channel_id=1, source_target_pairs={{8,0},{16,8},{24,16},{32,24},{40,32},{48,40},{56,48},{64,56},{72,6... | collective-permute-start | bytes 51848 | tf_op jit(solution)/shard_map/ppermute | solution.py:19
  480.2 136.2 %copy-start.7 = (f32[6,64,719]{2,0,1:T(8,128)S(1)}, f32[6,64,719]{2,0,1:T(8,128)}, u32[]{:S(2)}) copy-start(f32[6,64,719]{2,0,1:T(8,128)} %copy.203) | copy-start | bytes 3313156
  480.2 136.2 %copy-start.10 = (f32[6,63,720]{2,0,1:T(8,128)S(1)}, f32[6,63,720]{2,0,1:T(8,128)}, u32[]{:S(2)}) copy-start(f32[6,63,720]{2,0,1:T(8,128)} %slice.300) | copy-start | bytes 3265924
  480.2 136.2 %copy-start.19 = (f32[6,64,720]{2,1,0:T(8,128)S(1)}, f32[6,64,720]{2,1,0:T(8,128)}, u32[]{:S(2)}) copy-start(f32[6,64,720]{2,1,0:T(8,128)} %param.19) | copy-start | bytes 3317764
  480.2 136.2 %copy-start.22 = (f32[6,64,720]{2,1,0:T(8,128)S(1)}, f32[6,64,720]{2,1,0:T(8,128)}, u32[]{:S(2)}) copy-start(f32[6,64,720]{2,1,0:T(8,128)} %param.21) | copy-start | bytes 3317764
  480.7 135.7 %copy-start.4 = (f32[6,64,720]{2,0,1:T(8,128)S(1)}, f32[6,64,720]{2,0,1:T(8,128)}, u32[]{:S(2)}) copy-start(f32[6,64,720]{2,0,1:T(8,128)} %copy-done.2) | copy-start | bytes 3317764
  480.8 135.7 %copy-start.14 = (f32[6,64,720]{2,1,0:T(8,128)S(1)}, f32[6,64,720]{2,1,0:T(8,128)}, u32[]{:S(2)}) copy-start(f32[6,64,720]{2,1,0:T(8,128)} %param.20) | copy-start | bytes 3317764
  480.8 135.7 %copy-start.28 = (f32[1,64,720]{2,0,1:T(1,128)S(1)}, f32[1,64,720]{2,0,1:T(1,128)}, u32[]{:S(2)}) copy-start(f32[1,64,720]{2,0,1:T(1,128)} %broadcast_in_dim.90) | copy-start | bytes 552964
  606.0 7.6 %collective-permute-start.16 = (f32[1,66,720]{2,0,1:T(1,128)S(1)}, f32[1,66,720]{2,0,1:T(1,128)S(1)}, u32[]{:S(2)}, u32[]{:S(2)}) collective-permute-start(f32[1,66,720]{2,0,1:T(1,128)S(1)} %get-tuple-element.40), channel_id=1, source_target_pairs={{1,0},{2,1},{3,2},{4,3},{5,4},{6,5},{7,6},{9,8},{10,9},{11,10},{12... | collective-permute-start | bytes 570248 | tf_op jit(solution)/shard_map/ppermute | solution.py:19
  607.9 8.5 %collective-permute-start.17 = (f32[1,66,720]{2,0,1:T(1,128)S(1)}, f32[1,66,720]{2,0,1:T(1,128)S(1)}, u32[]{:S(2)}, u32[]{:S(2)}) collective-permute-start(f32[1,66,720]{2,0,1:T(1,128)S(1)} %get-tuple-element.41), channel_id=1, source_target_pairs={{0,1},{1,2},{2,3},{3,4},{4,5},{5,6},{6,7},{8,9},{9,10},{10,11},{11... | collective-permute-start | bytes 570248 | tf_op jit(solution)/shard_map/ppermute | solution.py:17
  (13 other events, 68.2 us)
Sparse Core Ops, SparseCore 0:
  27.5 104.6 reduce-scatter.3
  134.8 76.2 all-reduce.3
  382.4 75.7 all-reduce.5
